TPU v7x, 256 devices: a whole 4x4x8 slice. The times are simulated.
256 devices in a mesh: col: 32 (over x_hi, z, core), row: 8 (over x_lo, y).
Axes of the slice: x: 4 (x_hi: 2, x_lo: 2; x = x_hi * 2 + x_lo), y: 4, z: 8, core: 2. Of those that a mesh axis runs over, the one named last changes fastest.
Arguments:
- matrix: float32 [64, 64, 128, 128], P('col', 'row'), may hold values from -12 to 80, as said below
- col_owner: int32 [64], replicated, may hold values from 0 to 63, as said below
- row_owner: int32 [64], replicated, may hold values from 0 to 63, as said below
- pattern: int32 [2, 64], replicated, may hold values from 0 to 1, as said below
Outputs:
- factored: float32 [64, 64, 128, 128], P('col', 'row')
Inputs may be any that keep to these rules, and one draw needn't show every extreme that they name: `col_owner`: a permutation of 0 to 63. `row_owner`: a permutation of 0 to 63. pattern[0, 1] is 1; pattern[k, i] is 0 for i <= k; pattern[1, i] >= pattern[0, i] for every i >= 2. `matrix`: the diagonal tile of every supernode is symmetric positive definite, and so is every diagonal tile after the updates.
All inputs are finite; a program needn't handle non-finite values.
Results may differ from a plain program's by a relative error of at most 0.0003.
Values sent between devices are 32-bit elements; how exact they have to be, the bound alone decides.
A program may use at most 64 MiB of HBM per device.

v0:
```python
import jax
import jax.numpy as jnp
from jax import lax
from jax.sharding import PartitionSpec as P

PRECISE = lax.Precision.HIGHEST


def owned_nodes(owner_map, first_place, how_many):
    places = first_place + jnp.arange(how_many, dtype=jnp.int32)
    ordinal = jnp.arange(owner_map.shape[0], dtype=jnp.int32)
    matches = owner_map[None, :] == places[:, None]
    return jnp.sum(jnp.where(matches, ordinal[None, :], 0), axis=1)


def diag_factor(diag_tile):
    lower_tri = jnp.linalg.cholesky(diag_tile)
    identity = jnp.eye(lower_tri.shape[0], dtype=lower_tri.dtype)
    return (lower_tri, lax.linalg.triangular_solve(lower_tri, identity, left_side=True, lower=True))


def times_transposed(tiles, right):
    return jnp.einsum("...pq,rq->...pr", tiles, right, precision=PRECISE)


def keep_where(mask, tiles):
    return jnp.where(mask[..., None, None], tiles, jnp.zeros_like(tiles))


def body(matrix, col_owner, row_owner, pattern):
    cols_here = matrix.shape[0]
    slots_here = matrix.shape[1]
    col_rank = lax.axis_index("col")
    row_rank = lax.axis_index("row")
    first_slot = row_rank * slots_here
    col_node = owned_nodes(col_owner, col_rank * cols_here, cols_here)
    row_node = owned_nodes(row_owner, first_slot, slots_here)
    source_slot = row_owner[col_node]

    def own_tile(panel_id, slot):
        position = col_owner[panel_id]
        here = (position // cols_here == col_rank) & (slot // slots_here == row_rank)
        return keep_where(here, matrix[position % cols_here, slot % slots_here])

    leading = jnp.stack(
        [own_tile(0, row_owner[0]), own_tile(0, row_owner[1]), own_tile(1, row_owner[1])]
    )
    leading = lax.psum(leading, ("col", "row"))
    columns = jnp.stack(
        [
            keep_where(col_owner[k] // cols_here == col_rank, matrix[col_owner[k] % cols_here])
            for k in range(2)
        ]
    )
    columns, leading = lax.optimization_barrier((columns, leading))
    columns = lax.psum(columns, "col")
    held = source_slot // slots_here == row_rank
    across = keep_where(held[None, :], jnp.take(columns, source_slot % slots_here, axis=1))
    across = lax.psum(across, "row")
    lower_0, inverse_0 = diag_factor(leading[0])
    kept_next = jnp.where(pattern[0, 1] == 1, 1.0, 0.0).astype(jnp.float32)
    link = times_transposed(leading[1], inverse_0) * kept_next
    lower_1, inverse_1 = diag_factor(leading[2] - times_transposed(link, link))

    def factors(raw, nodes):
        kept = pattern[:, nodes] == 1
        first = keep_where(kept[0], times_transposed(raw[0], inverse_0))
        second = raw[1] - keep_where(nodes >= 1, times_transposed(first, link))
        second = keep_where(kept[1], times_transposed(second, inverse_1))
        return (first, second)

    row_factors = factors(columns, row_node)
    col_factors = factors(across, col_node)
    product = jnp.einsum(
        "spq,lrq->lspr",
        jnp.concatenate(row_factors, axis=-1),
        jnp.concatenate(col_factors, axis=-1),
        precision=PRECISE,
    )
    lower_half = row_node[None, :] >= col_node[:, None]
    matrix = matrix - keep_where(lower_half, product)
    for panel_id, lower_tri in enumerate((lower_0, lower_1)):
        mine = (col_node == panel_id)[:, None]
        is_diag = mine & (row_node == panel_id)[None, :]
        is_kept = mine & (pattern[panel_id][row_node] == 1)[None, :]
        matrix = jnp.where(is_kept[..., None, None], row_factors[panel_id][None], matrix)
        matrix = jnp.where(is_diag[..., None, None], lower_tri, matrix)
    return matrix


def solution(mesh):
    return jax.shard_map(
        body,
        mesh=mesh,
        in_specs=(P("col", "row", None, None), P(), P(), P()),
        out_specs=P("col", "row", None, None),
        check_vma=False,
    )
```

profile of v0, /device:TPU:4, one launch (start us, length us, event | category | flops | bytes accessed | tf_op | source)
XLA Modules:
  0.0 639.2 jit_solution(721035096207208400)
XLA Ops:
  6.5 0.7 copy-done.8
  7.2 0.7 fusion.39
  13.3 0.7 fusion.38
  19.4 1.6 copy.39
  21.1 0.7 pad_maximum_fusion.1
  21.8 0.2 fusion.30
  22.0 0.2 select_reduce_fusion.1
  22.3 0.6 slice.73
  23.0 0.6 gather_fusion.4
  23.6 0.1 copy.46
  23.7 0.9 dynamic-slice_select_fusion.1
  24.6 0.6 gather_fusion.3
  25.2 0.6 gather_fusion.1
  25.8 0.6 gather_fusion.2
  26.4 0.6 gather_fusion
  27.1 0.2 slice_reduce_fusion.1
  27.3 0.2 slice_reduce_fusion.2
  28.1 1.1 pad_maximum_fusion
  29.2 245.4 %all-reduce.4.cloned.1.call-done = f32[3,128,128]{1,2,0:T(8,128)} async-done(((f32[3,128,128]{1,2,0:T(8,128)}), f32[3,128,128]{1,2,0:T(8,128)}) %all-reduce.4.cloned.1.call-update) | async-done | bytes 196624 | tf_op jit(solution)/shard_map/psum | solution.py:48
  274.7 0.9 copy-done.6
  275.7 11.7 %cholesky.44 = f32[128,128]{1,0:T(8,128)S(1)} custom-call(f32[128,128]{1,0:T(8,128)S(1)} %fusion.15), custom_call_target="Cholesky" | custom-call | tf_op jit(solution)/shard_map/jit(cholesky)/cholesky | solution.py:17
  287.4 0.7 compare_reduce_fusion.1
  288.2 0.7 fusion.28
  288.9 9.8 %custom-call.6 = f32[1,128,128]{1,2,0:T(8,128)S(1)} custom-call(f32[1,128,128]{2,1,0:T(8,128)S(1)} %get-tuple-element.17), custom_call_target="InvertDiagBlocksLowerTriangular" | custom-call | tf_op jit(solution)/shard_map/triangular_solve/custom-call.0 | solution.py:19
  298.7 0.3 fusion.13
  299.0 0.3 convolution_multiply_fusion
  299.3 0.3 convolution_subtract_fusion
  299.5 0.1 copy.44
  299.7 11.7 %cholesky.55 = f32[128,128]{1,0:T(8,128)S(1)} custom-call(f32[128,128]{1,0:T(8,128)S(1)} %fusion.21), custom_call_target="Cholesky" | custom-call | tf_op jit(solution)/shard_map/jit(cholesky)/cholesky | solution.py:17
  311.4 0.7 compare_reduce_fusion
  312.1 0.7 select_bitcast_fusion.1
  312.8 10.0 %custom-call.7 = f32[1,128,128]{1,2,0:T(8,128)S(1)} custom-call(f32[1,128,128]{2,1,0:T(8,128)S(1)} %get-tuple-element.15), custom_call_target="InvertDiagBlocksLowerTriangular" | custom-call | tf_op jit(solution)/shard_map/triangular_solve/custom-call.0 | solution.py:19
  322.9 0.1 copy.50
  323.0 0.3 convolution_bitcast_fusion
  323.3 222.4 %all-reduce.6.cloned.1.call-done = f32[2,8,128,128]{3,2,1,0:T(8,128)} async-done(((f32[2,8,128,128]{3,2,1,0:T(8,128)}), f32[2,8,128,128]{3,2,1,0:T(8,128)}) %all-reduce.6.cloned.1.call-update) | async-done | bytes 1048592 | tf_op jit(solution)/shard_map/psum | solution.py:56
  545.7 1.9 gather_fusion.5
  547.6 0.8 select_bitcast_fusion
  548.5 0.6 convolution_select_fusion.3
  549.0 1.6 fusion.6
  550.7 1.0 copy.51
  551.7 0.6 convolution_select_fusion.1
  552.3 1.0 copy.49
  553.3 73.9 %all-reduce.8.cloned.1.call-done = f32[2,2,128,128]{3,2,0,1:T(8,128)} async-done(((f32[2,2,128,128]{3,2,0,1:T(8,128)}), f32[2,2,128,128]{3,2,0,1:T(8,128)}) %all-reduce.8.cloned.1.call-update) | async-done | bytes 262160 | tf_op jit(solution)/shard_map/psum | solution.py:59
  627.2 1.3 convolution_select_fusion.6
  628.5 1.2 fusion.7
  629.7 0.3 convolution_select_fusion.4
  630.0 1.4 fusion.5
  631.3 1.3 copy.56
  (48 shorter events, 0.7 us)
Async XLA Ops:
  6.5 0.7 copy-start.8
  6.5 268.1 %all-reduce.4.cloned.1.call-start = ((), (), s32[]{:S(2)}) async-start(), calls=%async_computation | async-start | bytes 393216 | tf_op jit(solution)/shard_map/psum | solution.py:48
  12.6 0.7 copy-start
  19.4 2.9 copy-start.7
  21.0 2.8 copy-start.1
  21.8 524.0 %all-reduce.6.cloned.1.call-start = ((), (), s32[]{:S(2)}) async-start(), calls=%async_computation.1 | async-start | bytes 2097152 | tf_op jit(solution)/shard_map/psum | solution.py:56
  25.7 2.4 copy-start.4
  274.6 0.9 copy-start.6
  274.7 352.5 %all-reduce.8.cloned.1.call-start = ((), (), s32[]{:S(2)}) async-start(), calls=%async_computation.2 | async-start | bytes 524288 | tf_op jit(solution)/shard_map/psum | solution.py:59
  545.7 2.7 copy-start.5
  627.2 2.8 copy-start.2
  627.2 2.8 copy-start.3
Sparse Core Ops, SparseCore 0:
  21.9 252.7 all-reduce.3
  277.3 268.4 all-reduce.5
  548.6 78.5 all-reduce.7
where the time goes:
time: 640 us; the launch traced here: 639 us
  waiting for transfers between devices  542 us (85%)
  other arithmetic  50.2 us (8%)
  between operations  25 us (4%)
  local copies, waits for them, and re-layouts  14.1 us (2%)
  matrix products  8.01 us (1%)
    psum x1, waiting for transfers between devices, body(): leading = lax.psum(leading, ('col', 'row'))  245 us
    psum x1, waiting for transfers between devices, body(): columns = lax.psum(columns, 'col')  222 us
    psum x1, waiting for transfers between devices, body(): across = lax.psum(across, 'row')  73.9 us
    another operation x6, other arithmetic, diag_factor(): lower_tri = jnp.linalg.cholesky(diag_tile)  24.9 us
    another operation x4, other arithmetic, diag_factor(): lax.linalg.triangular_solve(lower_tri, identity, left_side=True, lower=True)  21.2 us
  transfers between devices with their start and end apart: 3, of which 3 were waited for; matrix products, arithmetic and copies ran while one was open for 9% of the time, Pallas kernels for 0%

commit v1 on v0

--- a/solution.py
+++ b/solution.py
@@ -53,7 +53,7 @@
         ]
     )
     columns, leading = lax.optimization_barrier((columns, leading))
-    columns = lax.psum(columns, "col")
+    columns = jnp.sum(lax.all_gather(columns, "col"), axis=0)
     held = source_slot // slots_here == row_rank
     across = keep_where(held[None, :], jnp.take(columns, source_slot % slots_here, axis=1))
     across = lax.psum(across, "row")

time: 640 us -> 608 us (0.950)
  waiting for transfers between devices: 542 us -> 492 us
  other arithmetic: 50.2 us -> 64.4 us
    psum x1 -> x0, waiting for transfers between devices: 222 us -> none  [body(): columns = lax.psum(columns, 'col')]
    all_gather x0 -> x1, waiting for transfers between devices: none -> 166 us  [body(): columns = jnp.sum(lax.all_gather(columns, 'col'), axis=0)]
    reduce_sum x0 -> x1, other arithmetic: none -> 11.7 us  [body(): columns = jnp.sum(lax.all_gather(columns, 'col'), axis=0)]
  transfers between devices with their start and end apart: 3 -> 3, of which waited for: 3 -> 3; matrix products, arithmetic and copies ran while one was open for 9% -> 11% of each run, Pallas kernels for 0% -> 0%
where the time goes in v1:
time: 608 us; the launch traced here: 607 us
  waiting for transfers between devices  492 us (81%)
  other arithmetic  64.4 us (11%)
  between operations  24.9 us (4%)
  local copies, waits for them, and re-layouts  16.3 us (3%)
  matrix products  9.71 us (2%)
    psum x1, waiting for transfers between devices, body(): leading = lax.psum(leading, ('col', 'row'))  250 us
    all_gather x1, waiting for transfers between devices, body(): columns = jnp.sum(lax.all_gather(columns, 'col'), axis=0)  166 us
    psum x1, waiting for transfers between devices, body(): across = lax.psum(across, 'row')  75.4 us
    another operation x6, other arithmetic, diag_factor(): lower_tri = jnp.linalg.cholesky(diag_tile)  24.9 us
    another operation x4, other arithmetic, diag_factor(): lax.linalg.triangular_solve(lower_tri, identity, left_side=True, lower=True)  21.1 us
  transfers between devices with their start and end apart: 3, of which 3 were waited for; matrix products, arithmetic and copies ran while one was open for 11% of the time, Pallas kernels for 0%

profile of v1, /device:TPU:4, one launch (start us, length us, event | category | flops | bytes accessed | tf_op | source)
XLA Modules:
  0.0 607.5 jit_solution(14886651549431521953)
XLA Ops:
  6.5 1.4 fusion.39
  13.3 1.4 fusion.38
  20.1 1.6 copy.57
  21.8 0.7 pad_maximum_fusion.1
  22.6 1.3 dynamic-slice_select_fusion.1
  23.9 1.1 pad_maximum_fusion
  25.0 250.5 %all-reduce.3.cloned.1.call-done = f32[3,128,128]{1,2,0:T(8,128)} async-done(((f32[3,128,128]{1,2,0:T(8,128)}), f32[3,128,128]{1,2,0:T(8,128)}) %all-reduce.3.cloned.1.call-update) | async-done | bytes 196624 | tf_op jit(solution)/shard_map/psum | solution.py:48
  275.5 0.8 copy.64
  276.3 1.3 slice.73
  277.5 0.8 fusion.30
  278.4 1.3 gather_fusion.4
  279.7 0.6 gather_fusion.3
  280.3 0.8 select_reduce_fusion.1
  281.1 0.6 gather_fusion.1
  281.7 0.8 slice_bitcast_fusion.8
  282.4 0.6 gather_fusion.2
  283.1 0.6 gather_fusion
  284.4 0.2 slice_reduce_fusion.2
  284.5 0.2 slice_reduce_fusion.1
  284.9 0.8 slice_bitcast_fusion.6
  285.9 0.9 fusion.15
  286.7 11.7 %cholesky.44 = f32[128,128]{1,0:T(8,128)S(1)} custom-call(f32[128,128]{1,0:T(8,128)S(1)} %fusion.15), custom_call_target="Cholesky" | custom-call | tf_op jit(solution)/shard_map/jit(cholesky)/cholesky | solution.py:17
  298.5 0.7 compare_reduce_fusion.1
  299.2 0.7 fusion.28
  299.8 9.8 %custom-call.6 = f32[1,128,128]{1,2,0:T(8,128)S(1)} custom-call(f32[1,128,128]{2,1,0:T(8,128)S(1)} %get-tuple-element.17), custom_call_target="InvertDiagBlocksLowerTriangular" | custom-call | tf_op jit(solution)/shard_map/triangular_solve/custom-call.0 | solution.py:19
  309.6 0.3 fusion.13
  309.9 1.1 convolution_multiply_fusion
  311.1 1.1 convolution_subtract_fusion
  312.3 11.7 %cholesky.55 = f32[128,128]{1,0:T(8,128)S(1)} custom-call(f32[128,128]{1,0:T(8,128)S(1)} %fusion.21), custom_call_target="Cholesky" | custom-call | tf_op jit(solution)/shard_map/jit(cholesky)/cholesky | solution.py:17
  324.0 0.7 compare_reduce_fusion
  324.7 0.7 select_bitcast_fusion.1
  325.4 10.0 %custom-call.7 = f32[1,128,128]{1,2,0:T(8,128)S(1)} custom-call(f32[1,128,128]{2,1,0:T(8,128)S(1)} %get-tuple-element.15), custom_call_target="InvertDiagBlocksLowerTriangular" | custom-call | tf_op jit(solution)/shard_map/triangular_solve/custom-call.0 | solution.py:19
  335.6 0.3 convolution_bitcast_fusion
  335.9 166.3 %all-gather.3.cloned.1.call-done = f32[64,8,128,128]{3,2,1,0:T(8,128)} async-done(((f32[2,8,128,128]{3,2,1,0:T(8,128)}), f32[64,8,128,128]{3,2,1,0:T(8,128)}) %all-gather.3.cloned.1.call-update) | async-done | bytes 33554448 | tf_op jit(solution)/shard_map/all_gather | solution.py:56
  502.2 11.7 %reduce_sum.34 = f32[2,8,128,128]{3,2,1,0:T(8,128)S(1)} reduce(f32[32,2,8,128,128]{4,3,2,1,0:T(8,128)} %bitcast.115, f32[]{:T(128)} %constant.168.clone.1), dimensions={0}, to_apply=%region_5.8 | reduce | flops 8126464 | bytes 34603012 | tf_op jit(solution)/shard_map/reduce_sum | solution.py:56
  513.9 0.6 convolution_select_fusion.3
  514.5 0.6 gather_fusion.5
  515.1 0.8 select_bitcast_fusion
  515.9 0.6 fusion.6
  516.5 1.0 copy.69
  517.5 0.6 convolution_select_fusion.1
  518.1 1.0 copy.67
  519.1 75.4 %all-reduce.5.cloned.1.call-done = f32[2,2,128,128]{3,2,0,1:T(8,128)} async-done(((f32[2,2,128,128]{3,2,0,1:T(8,128)}), f32[2,2,128,128]{3,2,0,1:T(8,128)}) %all-reduce.5.cloned.1.call-update) | async-done | bytes 262160 | tf_op jit(solution)/shard_map/psum | solution.py:59
  594.5 1.2 convolution_select_fusion.6
  595.6 1.2 fusion.7
  596.8 0.3 convolution_select_fusion.4
  597.1 2.5 fusion.5
  599.6 1.3 copy.74
  (31 shorter events, 0.9 us)
Async XLA Ops:
  6.5 268.9 %all-reduce.3.cloned.1.call-start = ((), (), s32[]{:S(2)}) async-start(), calls=%async_computation | async-start | bytes 393216 | tf_op jit(solution)/shard_map/psum | solution.py:48
  22.5 479.7 %all-gather.3.cloned.1.call-start = ((), (), s32[]{:S(2)}) async-start(), calls=%async_computation.2 | async-start | bytes 34603008 | tf_op jit(solution)/shard_map/all_gather | solution.py:56
  275.4 319.0 %all-reduce.5.cloned.1.call-start = ((), (), s32[]{:S(2)}) async-start(), calls=%async_computation.1 | async-start | bytes 524288 | tf_op jit(solution)/shard_map/psum | solution.py:59
Sparse Core Ops, SparseCore 0:
  22.7 252.7 all-reduce.2
  278.2 223.9 all-gather.2
  516.0 78.3 all-reduce.4
